TPU v7x, 128 devices: a whole 4x4x4 slice. The times are simulated.
128 devices in a mesh: chord: 4 (over x_lo, core), normal: 32 (over x_hi, y, z).
Axes of the slice: x: 4 (x_hi: 2, x_lo: 2; x = x_hi * 2 + x_lo), y: 4, z: 4, core: 2. Of those that a mesh axis runs over, the one named last changes fastest.
Arguments:
- direct_modes: bfloat16 [16, 5, 64, 512, 256], P(None, None, 'chord', 'normal'), may hold values from -62 to 62
- adjoint_modes: bfloat16 [16, 5, 64, 512, 256], P(None, None, 'chord', 'normal'), may hold values from -5 to 5
- base_flow: float32 [5, 64, 512, 256], P(None, 'chord', 'normal'), may hold values from -5 to 5
- cell_type: int32 [64, 512, 256], P('chord', 'normal'), may hold values from 0 to 2
- mode_pick: int32 [16], replicated, may hold values from 0 to 15, each once
- flux_mix: float32 [3, 5, 5], replicated, may hold values from -2.5 to 2.5
Outputs:
- sensitivity: float32 [5, 64, 512, 256], P(None, 'chord', 'normal')
Inputs may be any that keep to these rules, and one draw needn't show every extreme that they name: `mode_pick`: each mode once.
All inputs are finite; a program needn't handle non-finite values.
Results may differ from a plain program's by a relative error of at most 0.0003.
Values may be sent and summed in bfloat16 or wider, within the bound.
A program may use at most 256 MiB of HBM per device.

v0:
```python
import jax
import jax.numpy as jnp
from jax import lax
from jax.sharding import PartitionSpec as P


def with_halo(cells, sides, width):
    for axis, dim in sides:
        count = lax.axis_size(axis)
        ends = count - 1
        head = lax.slice_in_dim(cells, 0, width, axis=dim)
        tail = lax.slice_in_dim(cells, cells.shape[dim] - width, cells.shape[dim], axis=dim)
        cells = jnp.concatenate(
            [
                lax.ppermute(tail, axis, [(i, (i + 1) % count) for i in range(ends)]),
                cells,
                lax.ppermute(head, axis, [((i + 1) % count, i) for i in range(ends)]),
            ],
            axis=dim,
        )
    return cells


def mixing(matrix, field_in):
    return jnp.einsum("ij,i...->j...", matrix, field_in, precision=lax.Precision.HIGHEST)


def diff_chord(padded):
    return padded[..., 2:, 1:-1, :] - padded[..., :-2, 1:-1, :]


def diff_normal(padded):
    return padded[..., 1:-1, 2:, :] - padded[..., 1:-1, :-2, :]


def inner_cells(padded):
    return padded[..., 1:-1, 1:-1, :]


def diff_span(field_in):
    return jnp.roll(field_in, -1, -1) - jnp.roll(field_in, 1, -1)


def bilinear_term(left_pad, right_pad, flux_mix):
    summed = jnp.zeros(inner_cells(left_pad).shape, jnp.float32)
    for axis_num, differ in ((0, diff_chord), (1, diff_normal)):
        mixed_adj = mixing(flux_mix[axis_num], right_pad)
        summed = summed + differ(left_pad) * inner_cells(mixed_adj) - differ(left_pad * mixed_adj)
    left_in = inner_cells(left_pad)
    mixed_adj = mixing(flux_mix[2], inner_cells(right_pad))
    return summed + diff_span(left_in) * mixed_adj - diff_span(left_in * mixed_adj)


def cell_weight(cell_type):
    return jnp.where(cell_type == 0, 1.0, jnp.where(cell_type == 1, 0.5, 0.0)).astype(jnp.float32)


def per_device(direct_modes, adjoint_modes, base_flow, cell_type, mode_pick, flux_mix):
    modes_count = direct_modes.shape[0]
    cells_all = direct_modes[0].size * lax.axis_size("chord") * lax.axis_size("normal")
    local_sums = jnp.sum(jnp.square(direct_modes.astype(jnp.float32)), axis=(1, 2, 3, 4))
    energy = lax.psum(local_sums, ("chord", "normal")) / cells_all
    amplitude = lax.rsqrt(energy + 1e-06)
    zeros_field = jnp.zeros(base_flow.shape, jnp.float32)
    direct_pad, adjoint_pad = (
        with_halo(direct_modes, (("chord", 2), ("normal", 3)), 1),
        with_halo(adjoint_modes, (("chord", 2), ("normal", 3)), 1),
    )

    def accumulate(number, summed):
        direct = direct_pad[number].astype(jnp.float32)
        adjoint = adjoint_pad[mode_pick[number]].astype(jnp.float32)
        return summed + amplitude[number] * bilinear_term(direct, adjoint, flux_mix)

    gradient = lax.fori_loop(0, modes_count, accumulate, zeros_field) / modes_count
    weight = cell_weight(cell_type)
    base_pad = with_halo(base_flow, (("chord", 1), ("normal", 2)), 1)

    def transpose_step(field_in):
        weighted = with_halo(weight * field_in, (("chord", 1), ("normal", 2)), 1)
        return bilinear_term(base_pad, weighted, flux_mix)

    once_applied = transpose_step(gradient)
    twice_applied = transpose_step(once_applied)
    return twice_applied


def solution(mesh):
    return jax.shard_map(
        per_device,
        mesh=mesh,
        in_specs=(
            P(None, None, "chord", "normal", None),
            P(None, None, "chord", "normal", None),
            P(None, "chord", "normal", None),
            P("chord", "normal", None),
            P(),
            P(),
        ),
        out_specs=P(None, "chord", "normal", None),
        check_vma=False,
    )
```

profile of v0, /device:TPU:121, one launch (start us, length us, event | category | flops | bytes accessed | tf_op | source)
XLA Modules:
  0.0 950.2 jit_solution(10213477555009542439)
XLA Ops:
  21.3 6.3 multiply_reduce_fusion
  31.0 62.0 %psum.7 = f32[16]{0:T(128)S(1)} all-reduce(f32[16]{0:T(128)S(1)} %multiply_reduce_fusion), channel_id=1, replica_groups=mesh['chord'=4,'normal'=32] {'chord','normal'}, use_global_device_ids=true, to_apply=%region_1.0 | all-reduce | flops 16 | bytes 128 | tf_op jit(solution)/shard_map/psum | solution.py:62
  100.5 19.8 %copy_dynamic-update-slice_fusion = bf16[16,5,18,16,256]{4,0,3,2,1:T(8,128)(2,1)} fusion(bf16[16,5,18,16,256]{4,0,3,2,1:T(8,128)(2,1)} %copy_dynamic-update-slice_fusion.4, bf16[16,5,16,16,256]{4,3,2,1,0:T(8,128)(2,1)} %param.9), kind=kLoop, calls=%fused_computation.41 | loop fusion | bytes 20971520
  124.0 6.3 collective-permute-start.8
  134.4 19.5 %copy_dynamic-update-slice_fusion.1 = bf16[16,5,18,16,256]{4,0,3,2,1:T(8,128)(2,1)} fusion(bf16[16,5,18,16,256]{4,0,3,2,1:T(8,128)(2,1)} %copy_dynamic-update-slice_fusion.6, bf16[16,5,16,16,256]{4,3,2,1,0:T(8,128)(2,1)} %param.8), kind=kLoop, calls=%fused_computation.42 | loop fusion | bytes 20971520
  157.5 9.1 collective-permute-start.4
  168.6 7.8 pad_maximum_fusion.1
  176.4 13.5 %copy.52 = bf16[16,5,18,18,256]{4,1,3,2,0:T(8,128)(2,1)} copy(bf16[16,5,18,18,256]{4,0,3,2,1:T(8,128)(2,1)S(1)} %pad_maximum_fusion.1) | data formatting | bytes 26542080
  193.9 13.6 %copy.51 = bf16[16,5,18,18,256]{4,1,3,2,0:T(8,128)(2,1)} copy(bf16[16,5,18,18,256]{4,0,3,2,1:T(8,128)(2,1)S(1)} %pad_maximum_fusion) | data formatting | bytes 26542080
  207.5 629.3 %while.14 = (s32[]{:T(128)}, f32[5,16,16,256]{3,0,2,1:T(8,128)}, f32[16]{0:T(128)S(1)}, bf16[16,5,18,18,256]{4,1,3,2,0:T(8,128)(2,1)}, s32[16]{0:T(128)S(1)}, /*...) while((s32[]{:T(128)}, f32[5,16,16,256]{3,0,2,1:T(8,128)}, ...), condition=%wide.region_3.4_spmd.clone, body=%wide.region_2.3_spmd.clone.sunk | while | flops 78295040 | bytes 61221592 | solution.py:75
  215.3 4.5 fusion.75
  225.1 7.6 convert_multiply_fusion.3
  233.4 12.8 %fusion.76 = f32[5,16,16,256]{3,0,2,1:T(8,128)} fusion(f32[5,18,18,256]{3,0,2,1:T(8,128)} %get-tuple-element.300, f32[5,18,18,256]{3,0,2,1:T(8,128)} %copy-done, f32[5,18,18,256]{3,0,2,1:T(8,128)S(1)} %bitcast_convert_fusion.2, f32[5,18,18,256]{3,0,2,1:T(8,128)} %get-tuple-element.301, f32[5,18,18,256]{3,0,2,1:T(8,128)} %get-tuple-element.302, ...), kind=kLoop, calls=%fused_computation.6.clone.1 | loop fusion | flops 6881280 | bytes 22282244 | tf_op jit(solution)/shard_map/while/body/eval_jaxpr/add | solution.py:73
  254.1 4.5 fusion.75
  263.9 7.6 convert_multiply_fusion.3
  272.1 13.4 %fusion.76 = f32[5,16,16,256]{3,0,2,1:T(8,128)} fusion(f32[5,18,18,256]{3,0,2,1:T(8,128)} %get-tuple-element.300, f32[5,18,18,256]{3,0,2,1:T(8,128)} %copy-done, f32[5,18,18,256]{3,0,2,1:T(8,128)S(1)} %bitcast_convert_fusion.2, f32[5,18,18,256]{3,0,2,1:T(8,128)} %get-tuple-element.301, f32[5,18,18,256]{3,0,2,1:T(8,128)} %get-tuple-element.302, ...), kind=kLoop, calls=%fused_computation.6.clone.1 | loop fusion | flops 6881280 | bytes 22282244 | tf_op jit(solution)/shard_map/while/body/eval_jaxpr/add | solution.py:73
  293.4 4.5 fusion.75
  303.2 7.6 convert_multiply_fusion.3
  311.5 13.4 %fusion.76 = f32[5,16,16,256]{3,0,2,1:T(8,128)} fusion(f32[5,18,18,256]{3,0,2,1:T(8,128)} %get-tuple-element.300, f32[5,18,18,256]{3,0,2,1:T(8,128)} %copy-done, f32[5,18,18,256]{3,0,2,1:T(8,128)S(1)} %bitcast_convert_fusion.2, f32[5,18,18,256]{3,0,2,1:T(8,128)} %get-tuple-element.301, f32[5,18,18,256]{3,0,2,1:T(8,128)} %get-tuple-element.302, ...), kind=kLoop, calls=%fused_computation.6.clone.1 | loop fusion | flops 6881280 | bytes 22282244 | tf_op jit(solution)/shard_map/while/body/eval_jaxpr/add | solution.py:73
  332.8 4.5 fusion.75
  342.6 7.6 convert_multiply_fusion.3
  350.9 13.4 %fusion.76 = f32[5,16,16,256]{3,0,2,1:T(8,128)} fusion(f32[5,18,18,256]{3,0,2,1:T(8,128)} %get-tuple-element.300, f32[5,18,18,256]{3,0,2,1:T(8,128)} %copy-done, f32[5,18,18,256]{3,0,2,1:T(8,128)S(1)} %bitcast_convert_fusion.2, f32[5,18,18,256]{3,0,2,1:T(8,128)} %get-tuple-element.301, f32[5,18,18,256]{3,0,2,1:T(8,128)} %get-tuple-element.302, ...), kind=kLoop, calls=%fused_computation.6.clone.1 | loop fusion | flops 6881280 | bytes 22282244 | tf_op jit(solution)/shard_map/while/body/eval_jaxpr/add | solution.py:73
  372.2 4.5 fusion.75
  381.9 7.6 convert_multiply_fusion.3
  390.2 13.4 %fusion.76 = f32[5,16,16,256]{3,0,2,1:T(8,128)} fusion(f32[5,18,18,256]{3,0,2,1:T(8,128)} %get-tuple-element.300, f32[5,18,18,256]{3,0,2,1:T(8,128)} %copy-done, f32[5,18,18,256]{3,0,2,1:T(8,128)S(1)} %bitcast_convert_fusion.2, f32[5,18,18,256]{3,0,2,1:T(8,128)} %get-tuple-element.301, f32[5,18,18,256]{3,0,2,1:T(8,128)} %get-tuple-element.302, ...), kind=kLoop, calls=%fused_computation.6.clone.1 | loop fusion | flops 6881280 | bytes 22282244 | tf_op jit(solution)/shard_map/while/body/eval_jaxpr/add | solution.py:73
  411.5 4.5 fusion.75
  421.3 7.6 convert_multiply_fusion.3
  429.6 13.4 %fusion.76 = f32[5,16,16,256]{3,0,2,1:T(8,128)} fusion(f32[5,18,18,256]{3,0,2,1:T(8,128)} %get-tuple-element.300, f32[5,18,18,256]{3,0,2,1:T(8,128)} %copy-done, f32[5,18,18,256]{3,0,2,1:T(8,128)S(1)} %bitcast_convert_fusion.2, f32[5,18,18,256]{3,0,2,1:T(8,128)} %get-tuple-element.301, f32[5,18,18,256]{3,0,2,1:T(8,128)} %get-tuple-element.302, ...), kind=kLoop, calls=%fused_computation.6.clone.1 | loop fusion | flops 6881280 | bytes 22282244 | tf_op jit(solution)/shard_map/while/body/eval_jaxpr/add | solution.py:73
  450.9 4.5 fusion.75
  460.7 7.6 convert_multiply_fusion.3
  468.9 13.4 %fusion.76 = f32[5,16,16,256]{3,0,2,1:T(8,128)} fusion(f32[5,18,18,256]{3,0,2,1:T(8,128)} %get-tuple-element.300, f32[5,18,18,256]{3,0,2,1:T(8,128)} %copy-done, f32[5,18,18,256]{3,0,2,1:T(8,128)S(1)} %bitcast_convert_fusion.2, f32[5,18,18,256]{3,0,2,1:T(8,128)} %get-tuple-element.301, f32[5,18,18,256]{3,0,2,1:T(8,128)} %get-tuple-element.302, ...), kind=kLoop, calls=%fused_computation.6.clone.1 | loop fusion | flops 6881280 | bytes 22282244 | tf_op jit(solution)/shard_map/while/body/eval_jaxpr/add | solution.py:73
  490.2 4.5 fusion.75
  500.0 7.6 convert_multiply_fusion.3
  508.3 13.4 %fusion.76 = f32[5,16,16,256]{3,0,2,1:T(8,128)} fusion(f32[5,18,18,256]{3,0,2,1:T(8,128)} %get-tuple-element.300, f32[5,18,18,256]{3,0,2,1:T(8,128)} %copy-done, f32[5,18,18,256]{3,0,2,1:T(8,128)S(1)} %bitcast_convert_fusion.2, f32[5,18,18,256]{3,0,2,1:T(8,128)} %get-tuple-element.301, f32[5,18,18,256]{3,0,2,1:T(8,128)} %get-tuple-element.302, ...), kind=kLoop, calls=%fused_computation.6.clone.1 | loop fusion | flops 6881280 | bytes 22282244 | tf_op jit(solution)/shard_map/while/body/eval_jaxpr/add | solution.py:73
  529.6 4.5 fusion.75
  539.4 7.6 convert_multiply_fusion.3
  547.7 13.4 %fusion.76 = f32[5,16,16,256]{3,0,2,1:T(8,128)} fusion(f32[5,18,18,256]{3,0,2,1:T(8,128)} %get-tuple-element.300, f32[5,18,18,256]{3,0,2,1:T(8,128)} %copy-done, f32[5,18,18,256]{3,0,2,1:T(8,128)S(1)} %bitcast_convert_fusion.2, f32[5,18,18,256]{3,0,2,1:T(8,128)} %get-tuple-element.301, f32[5,18,18,256]{3,0,2,1:T(8,128)} %get-tuple-element.302, ...), kind=kLoop, calls=%fused_computation.6.clone.1 | loop fusion | flops 6881280 | bytes 22282244 | tf_op jit(solution)/shard_map/while/body/eval_jaxpr/add | solution.py:73
  569.0 4.5 fusion.75
  578.7 7.6 convert_multiply_fusion.3
  587.0 13.4 %fusion.76 = f32[5,16,16,256]{3,0,2,1:T(8,128)} fusion(f32[5,18,18,256]{3,0,2,1:T(8,128)} %get-tuple-element.300, f32[5,18,18,256]{3,0,2,1:T(8,128)} %copy-done, f32[5,18,18,256]{3,0,2,1:T(8,128)S(1)} %bitcast_convert_fusion.2, f32[5,18,18,256]{3,0,2,1:T(8,128)} %get-tuple-element.301, f32[5,18,18,256]{3,0,2,1:T(8,128)} %get-tuple-element.302, ...), kind=kLoop, calls=%fused_computation.6.clone.1 | loop fusion | flops 6881280 | bytes 22282244 | tf_op jit(solution)/shard_map/while/body/eval_jaxpr/add | solution.py:73
  608.3 4.5 fusion.75
  618.1 7.6 convert_multiply_fusion.3
  626.4 13.4 %fusion.76 = f32[5,16,16,256]{3,0,2,1:T(8,128)} fusion(f32[5,18,18,256]{3,0,2,1:T(8,128)} %get-tuple-element.300, f32[5,18,18,256]{3,0,2,1:T(8,128)} %copy-done, f32[5,18,18,256]{3,0,2,1:T(8,128)S(1)} %bitcast_convert_fusion.2, f32[5,18,18,256]{3,0,2,1:T(8,128)} %get-tuple-element.301, f32[5,18,18,256]{3,0,2,1:T(8,128)} %get-tuple-element.302, ...), kind=kLoop, calls=%fused_computation.6.clone.1 | loop fusion | flops 6881280 | bytes 22282244 | tf_op jit(solution)/shard_map/while/body/eval_jaxpr/add | solution.py:73
  647.7 4.5 fusion.75
  657.5 7.6 convert_multiply_fusion.3
  665.7 13.4 %fusion.76 = f32[5,16,16,256]{3,0,2,1:T(8,128)} fusion(f32[5,18,18,256]{3,0,2,1:T(8,128)} %get-tuple-element.300, f32[5,18,18,256]{3,0,2,1:T(8,128)} %copy-done, f32[5,18,18,256]{3,0,2,1:T(8,128)S(1)} %bitcast_convert_fusion.2, f32[5,18,18,256]{3,0,2,1:T(8,128)} %get-tuple-element.301, f32[5,18,18,256]{3,0,2,1:T(8,128)} %get-tuple-element.302, ...), kind=kLoop, calls=%fused_computation.6.clone.1 | loop fusion | flops 6881280 | bytes 22282244 | tf_op jit(solution)/shard_map/while/body/eval_jaxpr/add | solution.py:73
  687.0 4.5 fusion.75
  696.8 7.6 convert_multiply_fusion.3
  705.1 13.4 %fusion.76 = f32[5,16,16,256]{3,0,2,1:T(8,128)} fusion(f32[5,18,18,256]{3,0,2,1:T(8,128)} %get-tuple-element.300, f32[5,18,18,256]{3,0,2,1:T(8,128)} %copy-done, f32[5,18,18,256]{3,0,2,1:T(8,128)S(1)} %bitcast_convert_fusion.2, f32[5,18,18,256]{3,0,2,1:T(8,128)} %get-tuple-element.301, f32[5,18,18,256]{3,0,2,1:T(8,128)} %get-tuple-element.302, ...), kind=kLoop, calls=%fused_computation.6.clone.1 | loop fusion | flops 6881280 | bytes 22282244 | tf_op jit(solution)/shard_map/while/body/eval_jaxpr/add | solution.py:73
  726.4 4.5 fusion.75
  736.2 7.6 convert_multiply_fusion.3
  744.5 13.4 %fusion.76 = f32[5,16,16,256]{3,0,2,1:T(8,128)} fusion(f32[5,18,18,256]{3,0,2,1:T(8,128)} %get-tuple-element.300, f32[5,18,18,256]{3,0,2,1:T(8,128)} %copy-done, f32[5,18,18,256]{3,0,2,1:T(8,128)S(1)} %bitcast_convert_fusion.2, f32[5,18,18,256]{3,0,2,1:T(8,128)} %get-tuple-element.301, f32[5,18,18,256]{3,0,2,1:T(8,128)} %get-tuple-element.302, ...), kind=kLoop, calls=%fused_computation.6.clone.1 | loop fusion | flops 6881280 | bytes 22282244 | tf_op jit(solution)/shard_map/while/body/eval_jaxpr/add | solution.py:73
  775.5 7.6 convert_multiply_fusion.3
  783.8 13.4 %fusion.76 = f32[5,16,16,256]{3,0,2,1:T(8,128)} fusion(f32[5,18,18,256]{3,0,2,1:T(8,128)} %get-tuple-element.300, f32[5,18,18,256]{3,0,2,1:T(8,128)} %copy-done, f32[5,18,18,256]{3,0,2,1:T(8,128)S(1)} %bitcast_convert_fusion.2, f32[5,18,18,256]{3,0,2,1:T(8,128)} %get-tuple-element.301, f32[5,18,18,256]{3,0,2,1:T(8,128)} %get-tuple-element.302, ...), kind=kLoop, calls=%fused_computation.6.clone.1 | loop fusion | flops 6881280 | bytes 22282244 | tf_op jit(solution)/shard_map/while/body/eval_jaxpr/add | solution.py:73
  814.9 7.6 convert_multiply_fusion.3
  823.2 13.4 %fusion.76 = f32[5,16,16,256]{3,0,2,1:T(8,128)} fusion(f32[5,18,18,256]{3,0,2,1:T(8,128)} %get-tuple-element.300, f32[5,18,18,256]{3,0,2,1:T(8,128)} %copy-done, f32[5,18,18,256]{3,0,2,1:T(8,128)S(1)} %bitcast_convert_fusion.2, f32[5,18,18,256]{3,0,2,1:T(8,128)} %get-tuple-element.301, f32[5,18,18,256]{3,0,2,1:T(8,128)} %get-tuple-element.302, ...), kind=kLoop, calls=%fused_computation.6.clone.1 | loop fusion | flops 6881280 | bytes 22282244 | tf_op jit(solution)/shard_map/while/body/eval_jaxpr/add | solution.py:73
  858.4 7.1 collective-permute-start.12
  867.4 9.1 collective-permute-start.14
  881.1 7.1 collective-permute-done.15
  888.1 5.4 fusion.40
  893.6 9.5 %fusion.32 = f32[5,16,16,256]{3,0,2,1:T(8,128)S(1)} fusion(f32[5,18,18,256]{3,0,2,1:T(8,128)} %get-tuple-element.210, f32[5,18,18,256]{3,0,2,1:T(8,128)} %copy-done.10, f32[5,18,18,256]{3,0,2,1:T(8,128)} %get-tuple-element.209, f32[5,18,18,256]{3,0,2,1:T(8,128)} %get-tuple-element.240, f32[5,16,16,1]{3,0,2,1:T(8,128)} %get-tuple-element.228, ...), kind=kLoop, calls=%fused_computation.59 | loop fusion | flops 7536640 | bytes 19124224 | tf_op jit(solution)/shard_map/mul | solution.py:80
  922.6 9.1 collective-permute-done.19
  934.2 5.5 fusion.38
  939.6 8.6 fusion.26
  (239 shorter events, 299.0 us)
Async XLA Ops:
  0.0 16.0 %copy-start.4 = (f32[5,16,16,256]{3,2,1,0:T(8,128)S(1)}, f32[5,16,16,256]{3,2,1,0:T(8,128)}, u32[]{:S(2)}) copy-start(f32[5,16,16,256]{3,2,1,0:T(8,128)} %param.10) | copy-start | bytes 3932164
  2.3 96.0 %collective-permute-start.6 = (bf16[16,5,1,16,256]{4,3,2,1,0:T(8,128)(2,1)}, bf16[16,5,1,16,256]{4,3,2,1,0:T(8,128)(2,1)}, u32[]{:S(2)}, u32[]{:S(2)}) collective-permute-start(bf16[16,5,1,16,256]{4,3,2,1,0:T(8,128)(2,1)} %get-tuple-element.204), channel_id=1, source_target_pairs={{0,32},{32,64},{64,96},{1,33},{33,65},{65,97},{2,34},{34,66},{66,9... | collective-permute-start | bytes 1966088 | tf_op jit(solution)/shard_map/ppermute | solution.py:15
  6.0 114.3 %collective-permute-start.7 = (bf16[16,5,1,16,256]{4,3,2,1,0:T(8,128)(2,1)S(1)}, bf16[16,5,1,16,256]{4,3,2,1,0:T(8,128)(2,1)}, u32[]{:S(2)}, u32[]{:S(2)}) collective-permute-start(bf16[16,5,1,16,256]{4,3,2,1,0:T(8,128)(2,1)S(1)} %get-tuple-element.203), channel_id=1, source_target_pairs={{32,0},{64,32},{96,64},{33,1},{65,33},{97,65},{34,2},{66,34},{98,6... | collective-permute-start | bytes 1966088 | tf_op jit(solution)/shard_map/ppermute | solution.py:17
  10.4 121.8 %collective-permute-start.2 = (bf16[16,5,1,16,256]{4,3,2,1,0:T(8,128)(2,1)}, bf16[16,5,1,16,256]{4,3,2,1,0:T(8,128)(2,1)}, u32[]{:S(2)}, u32[]{:S(2)}) collective-permute-start(bf16[16,5,1,16,256]{4,3,2,1,0:T(8,128)(2,1)} %get-tuple-element.206), channel_id=1, source_target_pairs={{0,32},{32,64},{64,96},{1,33},{33,65},{65,97},{2,34},{34,66},{66,9... | collective-permute-start | bytes 1966088 | tf_op jit(solution)/shard_map/ppermute | solution.py:15
  14.1 139.8 %collective-permute-start.3 = (bf16[16,5,1,16,256]{4,3,2,1,0:T(8,128)(2,1)}, bf16[16,5,1,16,256]{4,3,2,1,0:T(8,128)(2,1)}, u32[]{:S(2)}, u32[]{:S(2)}) collective-permute-start(bf16[16,5,1,16,256]{4,3,2,1,0:T(8,128)(2,1)} %get-tuple-element.205), channel_id=1, source_target_pairs={{32,0},{64,32},{96,64},{33,1},{65,33},{97,65},{34,2},{66,34},{98,6... | collective-permute-start | bytes 1966088 | tf_op jit(solution)/shard_map/ppermute | solution.py:17
  16.9 76.2 %copy-start.1 = (f32[5,16,16,256]{3,0,2,1:T(8,128)}, f32[5,16,16,256]{3,0,2,1:T(8,128)S(1)}, u32[]{:S(2)}) copy-start(f32[5,16,16,256]{3,0,2,1:T(8,128)S(1)} %copy.42) | copy-start | bytes 3932164
  17.6 77.2 %collective-permute-start.1 = (f32[5,1,16,256]{3,0,2,1:T(8,128)S(1)}, f32[5,1,16,256]{3,0,2,1:T(8,128)S(1)}, u32[]{:S(2)}, u32[]{:S(2)}) collective-permute-start(f32[5,1,16,256]{3,0,2,1:T(8,128)S(1)} %get-tuple-element.232), channel_id=1, source_target_pairs={{0,32},{32,64},{64,96},{1,33},{33,65},{65,97},{2,34},{34,66},{66,9... | collective-permute-start | bytes 245768 | tf_op jit(solution)/shard_map/ppermute | solution.py:15
  27.5 2.7 copy-start.15
  93.1 1.7 copy-start.16
  94.8 25.5 %copy-start.12 = (f32[5,1,16,256]{3,0,2,1:T(8,128)}, f32[5,1,16,256]{3,0,2,1:T(8,128)S(1)}, u32[]{:S(2)}) copy-start(f32[5,1,16,256]{3,0,2,1:T(8,128)S(1)} %collective-permute-done.1) | copy-start | bytes 245764
  94.8 759.2 %collective-permute-start = (f32[5,1,16,256]{3,0,2,1:T(8,128)}, f32[5,1,16,256]{3,0,2,1:T(8,128)}, u32[]{:S(2)}, u32[]{:S(2)}) collective-permute-start(f32[5,1,16,256]{3,0,2,1:T(8,128)} %get-tuple-element.231), channel_id=1, source_target_pairs={{32,0},{64,32},{96,64},{33,1},{65,33},{97,65},{34,2},{66,34},{98,6... | collective-permute-start | bytes 245768 | tf_op jit(solution)/shard_map/ppermute | solution.py:17
  124.0 44.6 %collective-permute-start.8 = (bf16[16,5,18,1,256]{4,0,3,2,1:T(8,128)(2,1)S(1)}, bf16[16,5,18,1,256]{4,0,3,2,1:T(8,128)(2,1)S(1)}, u32[]{:S(2)}, u32[]{:S(2)}) collective-permute-start(bf16[16,5,18,1,256]{4,0,3,2,1:T(8,128)(2,1)S(1)} %get-tuple-element.199), channel_id=1, source_target_pairs={{0,1},{1,2},{2,3},{3,4},{4,5},{5,6},{6,7},{7,8},{8,9},{9,10},{10,1... | collective-permute-start | bytes 2211848 | tf_op jit(solution)/shard_map/ppermute | solution.py:15
  130.3 38.3 %collective-permute-start.9 = (bf16[16,5,18,1,256]{4,0,3,2,1:T(8,128)(2,1)S(1)}, bf16[16,5,18,1,256]{4,0,3,2,1:T(8,128)(2,1)S(1)}, u32[]{:S(2)}, u32[]{:S(2)}) collective-permute-start(bf16[16,5,18,1,256]{4,0,3,2,1:T(8,128)(2,1)S(1)} %get-tuple-element.200), channel_id=1, source_target_pairs={{1,0},{2,1},{3,2},{4,3},{5,4},{6,5},{7,6},{8,7},{9,8},{10,9},{11,1... | collective-permute-start | bytes 2211848 | tf_op jit(solution)/shard_map/ppermute | solution.py:17
  157.5 32.4 %collective-permute-start.4 = (bf16[16,5,18,1,256]{4,0,3,2,1:T(8,128)(2,1)S(1)}, bf16[16,5,18,1,256]{4,0,3,2,1:T(8,128)(2,1)S(1)}, u32[]{:S(2)}, u32[]{:S(2)}) collective-permute-start(bf16[16,5,18,1,256]{4,0,3,2,1:T(8,128)(2,1)S(1)} %get-tuple-element.201), channel_id=1, source_target_pairs={{0,1},{1,2},{2,3},{3,4},{4,5},{5,6},{6,7},{7,8},{8,9},{9,10},{10,1... | collective-permute-start | bytes 2211848 | tf_op jit(solution)/shard_map/ppermute | solution.py:15
  166.6 25.5 %collective-permute-start.5 = (bf16[16,5,18,1,256]{4,0,3,2,1:T(8,128)(2,1)S(1)}, bf16[16,5,18,1,256]{4,0,3,2,1:T(8,128)(2,1)S(1)}, u32[]{:S(2)}, u32[]{:S(2)}) collective-permute-start(bf16[16,5,18,1,256]{4,0,3,2,1:T(8,128)(2,1)S(1)} %get-tuple-element.202), channel_id=1, source_target_pairs={{1,0},{2,1},{3,2},{4,3},{5,4},{6,5},{7,6},{8,7},{9,8},{10,9},{11,1... | collective-permute-start | bytes 2211848 | tf_op jit(solution)/shard_map/ppermute | solution.py:17
  168.6 23.5 %slice-start = ((s8[11796480]{0:T(1024)(128)(4,1)}), s8[4194304]{0:T(1024)(128)(4,1)S(1)}, s32[]{:S(2)}) async-start(s8[11796480]{0:T(1024)(128)(4,1)} %bitcast.119), calls=%async_computation | async-start | bytes 8388608
  168.6 23.5 %slice-start.1 = ((s8[11796480]{0:T(1024)(128)(4,1)}), s8[4194304]{0:T(1024)(128)(4,1)S(1)}, s32[]{:S(2)}) async-start(s8[11796480]{0:T(1024)(128)(4,1)} %bitcast.119), calls=%async_computation.1 | async-start | bytes 8388608
  176.4 15.7 %slice-start.2 = ((s8[11796480]{0:T(1024)(128)(4,1)}), s8[3407872]{0:T(1024)(128)(4,1)S(1)}, s32[]{:S(2)}) async-start(s8[11796480]{0:T(1024)(128)(4,1)} %bitcast.119), calls=%async_computation.2 | async-start | bytes 6815744
  193.9 13.6 %copy-start.17 = (s32[16]{0:T(128)S(1)}, s32[16]{0:T(128)}, u32[]{:S(2)}) copy-start(s32[16]{0:T(128)} %param.12) | copy-start | bytes 196
  207.5 629.4 %copy-start.14 = (f32[16,16,256]{2,1,0:T(8,128)S(1)}, f32[16,16,256]{2,1,0:T(8,128)}, u32[]{:S(2)}) copy-start(f32[16,16,256]{2,1,0:T(8,128)} %get-tuple-element.238) | copy-start | bytes 786436
  225.1 7.6 copy-start
  263.8 7.6 copy-start
  303.2 7.6 copy-start
  342.6 7.6 copy-start
  381.9 7.6 copy-start
  421.3 7.6 copy-start
  460.6 7.6 copy-start
  500.0 7.6 copy-start
  539.4 7.6 copy-start
  578.7 7.6 copy-start
  618.1 7.6 copy-start
  657.4 7.6 copy-start
  696.8 7.6 copy-start
  736.2 7.6 copy-start
  775.5 7.6 copy-start
  814.9 7.6 copy-start
  836.8 2.3 copy-start.3
  836.8 2.6 copy-start.5
  848.0 7.0 collective-permute-start.10
  852.1 6.3 collective-permute-start.11
  858.4 20.1 %collective-permute-start.12 = (f32[5,18,1,256]{3,0,2,1:T(8,128)S(1)}, f32[5,18,1,256]{3,0,2,1:T(8,128)S(1)}, u32[]{:S(2)}, u32[]{:S(2)}) collective-permute-start(f32[5,18,1,256]{3,0,2,1:T(8,128)S(1)} %get-tuple-element.215), channel_id=1, source_target_pairs={{0,1},{1,2},{2,3},{3,4},{4,5},{5,6},{6,7},{7,8},{8,9},{9,10},{10,1... | collective-permute-start | bytes 276488 | tf_op jit(solution)/shard_map/ppermute | solution.py:15
  865.5 13.0 %collective-permute-start.13 = (f32[5,18,1,256]{3,0,2,1:T(8,128)S(1)}, f32[5,18,1,256]{3,0,2,1:T(8,128)S(1)}, u32[]{:S(2)}, u32[]{:S(2)}) collective-permute-start(f32[5,18,1,256]{3,0,2,1:T(8,128)S(1)} %get-tuple-element.216), channel_id=1, source_target_pairs={{1,0},{2,1},{3,2},{4,3},{5,4},{6,5},{7,6},{8,7},{9,8},{10,9},{11,1... | collective-permute-start | bytes 276488 | tf_op jit(solution)/shard_map/ppermute | solution.py:17
  867.4 13.6 %collective-permute-start.14 = (f32[5,18,1,256]{3,0,2,1:T(8,128)S(1)}, f32[5,18,1,256]{3,0,2,1:T(8,128)S(1)}, u32[]{:S(2)}, u32[]{:S(2)}) collective-permute-start(f32[5,18,1,256]{3,0,2,1:T(8,128)S(1)} %get-tuple-element.213), channel_id=1, source_target_pairs={{0,1},{1,2},{2,3},{3,4},{4,5},{5,6},{6,7},{7,8},{8,9},{9,10},{10,1... | collective-permute-start | bytes 276488 | tf_op jit(solution)/shard_map/ppermute | solution.py:15
  876.5 11.6 %collective-permute-start.15 = (f32[5,18,1,256]{3,0,2,1:T(8,128)S(1)}, f32[5,18,1,256]{3,0,2,1:T(8,128)S(1)}, u32[]{:S(2)}, u32[]{:S(2)}) collective-permute-start(f32[5,18,1,256]{3,0,2,1:T(8,128)S(1)} %get-tuple-element.214), channel_id=1, source_target_pairs={{1,0},{2,1},{3,2},{4,3},{5,4},{6,5},{7,6},{8,7},{9,8},{10,9},{11,1... | collective-permute-start | bytes 276488 | tf_op jit(solution)/shard_map/ppermute | solution.py:17
  881.0 12.6 %copy-start.10 = (f32[5,18,18,256]{3,0,2,1:T(8,128)}, f32[5,18,18,256]{3,0,2,1:T(8,128)S(1)}, u32[]{:S(2)}) copy-start(f32[5,18,18,256]{3,0,2,1:T(8,128)S(1)} %convolution_bitcast_fusion.4) | copy-start | bytes 4976644
  881.0 12.6 %copy-start.2 = (f32[5,16,16,256]{3,0,2,1:T(8,128)S(1)}, f32[5,16,16,256]{3,0,2,1:T(8,128)}, u32[]{:S(2)}) copy-start(f32[5,16,16,256]{3,0,2,1:T(8,128)} %copy-done.1) | copy-start | bytes 3932164
  881.0 12.5 %copy-start.6 = (f32[5,16,16,255]{3,0,2,1:T(8,128)S(1)}, f32[5,16,16,255]{3,0,2,1:T(8,128)}, u32[]{:S(2)}) copy-start(f32[5,16,16,255]{3,0,2,1:T(8,128)} %get-tuple-element.223) | copy-start | bytes 3916804
  881.0 12.5 %copy-start.7 = (f32[5,16,16,255]{3,0,2,1:T(8,128)S(1)}, f32[5,16,16,255]{3,0,2,1:T(8,128)}, u32[]{:S(2)}) copy-start(f32[5,16,16,255]{3,0,2,1:T(8,128)} %get-tuple-element.224) | copy-start | bytes 3916804
  881.0 12.5 %copy-start.8 = (f32[5,16,16,1]{3,0,2,1:T(8,128)S(1)}, f32[5,16,16,1]{3,0,2,1:T(8,128)}, u32[]{:S(2)}) copy-start(f32[5,16,16,1]{3,0,2,1:T(8,128)} %get-tuple-element.225) | copy-start | bytes 15364
  881.0 12.5 %copy-start.9 = (f32[5,16,16,1]{3,0,2,1:T(8,128)S(1)}, f32[5,16,16,1]{3,0,2,1:T(8,128)}, u32[]{:S(2)}) copy-start(f32[5,16,16,1]{3,0,2,1:T(8,128)} %get-tuple-element.226) | copy-start | bytes 15364
  881.0 12.5 %copy-start.13 = (f32[5,1,16,256]{3,0,2,1:T(8,128)S(1)}, f32[5,1,16,256]{3,0,2,1:T(8,128)}, u32[]{:S(2)}) copy-start(f32[5,1,16,256]{3,0,2,1:T(8,128)} %copy-done.12) | copy-start | bytes 245764
  907.2 7.8 collective-permute-start.16
  910.4 6.3 collective-permute-start.17
  916.7 5.9 collective-permute-start.18
  920.1 11.6 %collective-permute-start.19 = (f32[5,18,1,256]{3,0,2,1:T(8,128)S(1)}, f32[5,18,1,256]{3,0,2,1:T(8,128)S(1)}, u32[]{:S(2)}, u32[]{:S(2)}) collective-permute-start(f32[5,18,1,256]{3,0,2,1:T(8,128)S(1)} %get-tuple-element.212), channel_id=1, source_target_pairs={{1,0},{2,1},{3,2},{4,3},{5,4},{6,5},{7,6},{8,7},{9,8},{10,9},{11,1... | collective-permute-start | bytes 276488 | tf_op jit(solution)/shard_map/ppermute | solution.py:17
  934.2 5.5 copy-start.11
where the time goes:
time: 959 us; the launch traced here: 950 us
  other arithmetic  277 us (29%)
  matrix products  247 us (26%)
  local copies, waits for them, and re-layouts  235 us (25%)
  starting transfers between devices  73.2 us (8%)
  blocking collectives  62 us (6%)
  loops' own time  32 us (3%)
  waiting for transfers between devices  23.7 us (2%)
    dot_general x54, matrix products, mixing(): jnp.einsum('ij,i...->j...', matrix, field_in, precision=lax.Precision.HIG...  247 us
    add x16, other arithmetic, accumulate(): return summed + amplitude[number] * bilinear_term(direct, adjoint, flux_mix)  214 us
    slice x38, local copies, waits for them, and re-layouts, diff_span(): return jnp.roll(field_in, -1, -1) - jnp.roll(field_in, 1, -1)  127 us
    unnamed x49, local copies, waits for them, and re-layouts  73 us
    psum x1, blocking collectives, per_device(): energy = lax.psum(local_sums, ('chord', 'normal')) / cells_all  62 us
    ppermute x10, starting transfers between devices, with_halo(): lax.ppermute(tail, axis, [(i, (i + 1) % count) for i in range(ends)])  53.1 us
    another operation x1, loops' own time, per_device(): lax.fori_loop(0, modes_count, accumulate, zeros_field) / modes_count  32 us
    convert_element_type x16, other arithmetic, accumulate(): direct = direct_pad[number].astype(jnp.float32)  25.6 us
  transfers between devices with their start and end apart: 20, of which 6 were waited for; matrix products, arithmetic and copies ran while one was open for 76% of the time, Pallas kernels for 0%

commit v1 on v0

--- a/solution.py
+++ b/solution.py
@@ -59,7 +59,7 @@
     modes_count = direct_modes.shape[0]
     cells_all = direct_modes[0].size * lax.axis_size("chord") * lax.axis_size("normal")
     local_sums = jnp.sum(jnp.square(direct_modes.astype(jnp.float32)), axis=(1, 2, 3, 4))
-    energy = lax.psum(local_sums, ("chord", "normal")) / cells_all
+    energy = lax.psum(lax.psum(local_sums, "chord"), "normal") / cells_all
     amplitude = lax.rsqrt(energy + 1e-06)
     zeros_field = jnp.zeros(base_flow.shape, jnp.float32)
     direct_pad, adjoint_pad = (

time: 959 us -> 995 us (1.038)
  starting transfers between devices: 73.2 us -> 91.4 us
  blocking collectives: 62 us -> 79.8 us
    psum x1 -> x2, blocking collectives: 62 us -> 79.8 us  [per_device(): energy = lax.psum(lax.psum(local_sums, 'chord'), 'normal') / cells_all]
    ppermute x10, starting transfers between devices: 20.1 us -> 34.4 us  [with_halo(): lax.ppermute(head, axis, [((i + 1) % count, i) for i in range(ends)])]
  transfers between devices with their start and end apart: 20 -> 20, of which waited for: 6 -> 6; matrix products, arithmetic and copies ran while one was open for 76% -> 73% of each run, Pallas kernels for 0% -> 0%
where the time goes in v1:
time: 995 us; the launch traced here: 987 us
  other arithmetic  277 us (28%)
  matrix products  247 us (25%)
  local copies, waits for them, and re-layouts  235 us (24%)
  starting transfers between devices  91.4 us (9%)
  blocking collectives  79.8 us (8%)
  loops' own time  32 us (3%)
  waiting for transfers between devices  23.7 us (2%)
    dot_general x54, matrix products, mixing(): jnp.einsum('ij,i...->j...', matrix, field_in, precision=lax.Precision.HIG...  247 us
    add x16, other arithmetic, accumulate(): return summed + amplitude[number] * bilinear_term(direct, adjoint, flux_mix)  215 us
    slice x38, local copies, waits for them, and re-layouts, diff_span(): return jnp.roll(field_in, -1, -1) - jnp.roll(field_in, 1, -1)  127 us
    psum x2, blocking collectives, per_device(): energy = lax.psum(lax.psum(local_sums, 'chord'), 'normal') / cells_all  79.8 us
    unnamed x49, local copies, waits for them, and re-layouts  72.9 us
    ppermute x10, starting transfers between devices, with_halo(): lax.ppermute(tail, axis, [(i, (i + 1) % count) for i in range(ends)])  57 us
    ppermute x10, starting transfers between devices, with_halo(): lax.ppermute(head, axis, [((i + 1) % count, i) for i in range(ends)])  34.4 us
    another operation x1, loops' own time, per_device(): lax.fori_loop(0, modes_count, accumulate, zeros_field) / modes_count  32 us
  transfers between devices with their start and end apart: 20, of which 6 were waited for; matrix products, arithmetic and copies ran while one was open for 73% of the time, Pallas kernels for 0%

profile of v1, /device:TPU:121, one launch (start us, length us, event | category | flops | bytes accessed | tf_op | source)
XLA Modules:
  0.0 986.9 jit_solution(4055199788733194019)
XLA Ops:
  21.3 6.3 multiply_reduce_fusion
  31.1 5.1 psum.14
  36.2 74.7 %psum.15 = f32[16]{0:T(128)S(1)} all-reduce(f32[16]{0:T(128)S(1)} %psum.14), channel_id=1, replica_groups=mesh['chord'=4,'normal'=32] {'normal'}, use_global_device_ids=true, to_apply=%region_2.0 | all-reduce | flops 16 | bytes 128 | tf_op jit(solution)/shard_map/psum | solution.py:62
  112.6 17.1 %collective-permute-start = (f32[5,1,16,256]{3,0,2,1:T(8,128)}, f32[5,1,16,256]{3,0,2,1:T(8,128)}, u32[]{:S(2)}, u32[]{:S(2)}) collective-permute-start(f32[5,1,16,256]{3,0,2,1:T(8,128)} %get-tuple-element.231), channel_id=1, source_target_pairs={{32,0},{64,32},{96,64},{33,1},{65,33},{97,65},{34,2},{66,34},{98,6... | collective-permute-start | bytes 245768 | tf_op jit(solution)/shard_map/ppermute | solution.py:17
  132.5 19.8 %copy_dynamic-update-slice_fusion = bf16[16,5,18,16,256]{4,0,3,2,1:T(8,128)(2,1)} fusion(bf16[16,5,18,16,256]{4,0,3,2,1:T(8,128)(2,1)} %copy_dynamic-update-slice_fusion.4, bf16[16,5,16,16,256]{4,3,2,1,0:T(8,128)(2,1)} %param.9), kind=kLoop, calls=%fused_computation.41 | loop fusion | bytes 20971520
  156.0 9.6 collective-permute-start.8
  169.7 19.5 %copy_dynamic-update-slice_fusion.1 = bf16[16,5,18,16,256]{4,0,3,2,1:T(8,128)(2,1)} fusion(bf16[16,5,18,16,256]{4,0,3,2,1:T(8,128)(2,1)} %copy_dynamic-update-slice_fusion.6, bf16[16,5,16,16,256]{4,3,2,1,0:T(8,128)(2,1)} %param.8), kind=kLoop, calls=%fused_computation.42 | loop fusion | bytes 20971520
  192.8 9.1 collective-permute-start.4
  203.8 7.8 pad_maximum_fusion.1
  211.6 13.5 %copy.52 = bf16[16,5,18,18,256]{4,1,3,2,0:T(8,128)(2,1)} copy(bf16[16,5,18,18,256]{4,0,3,2,1:T(8,128)(2,1)S(1)} %pad_maximum_fusion.1) | data formatting | bytes 26542080
  229.1 13.5 %copy.51 = bf16[16,5,18,18,256]{4,1,3,2,0:T(8,128)(2,1)} copy(bf16[16,5,18,18,256]{4,0,3,2,1:T(8,128)(2,1)S(1)} %pad_maximum_fusion) | data formatting | bytes 26542080
  242.7 630.4 %while.14 = (s32[]{:T(128)}, f32[5,16,16,256]{3,0,2,1:T(8,128)}, f32[16]{0:T(128)S(1)}, bf16[16,5,18,18,256]{4,1,3,2,0:T(8,128)(2,1)}, s32[16]{0:T(128)S(1)}, /*...) while((s32[]{:T(128)}, f32[5,16,16,256]{3,0,2,1:T(8,128)}, ...), condition=%wide.region_4.5_spmd.clone, body=%wide.region_3.4_spmd.clone.sunk | while | flops 78295040 | bytes 61221592 | solution.py:75
  250.5 4.5 fusion.75
  260.3 7.6 convert_multiply_fusion.3
  268.6 12.9 %fusion.76 = f32[5,16,16,256]{3,0,2,1:T(8,128)} fusion(f32[5,18,18,256]{3,0,2,1:T(8,128)} %get-tuple-element.300, f32[5,18,18,256]{3,0,2,1:T(8,128)} %copy-done, f32[5,18,18,256]{3,0,2,1:T(8,128)S(1)} %bitcast_convert_fusion.2, f32[5,18,18,256]{3,0,2,1:T(8,128)} %get-tuple-element.301, f32[5,18,18,256]{3,0,2,1:T(8,128)} %get-tuple-element.302, ...), kind=kLoop, calls=%fused_computation.6.clone.1 | loop fusion | flops 6881280 | bytes 22282244 | tf_op jit(solution)/shard_map/while/body/eval_jaxpr/add | solution.py:73
  289.4 4.5 fusion.75
  299.1 7.6 convert_multiply_fusion.3
  307.4 13.5 %fusion.76 = f32[5,16,16,256]{3,0,2,1:T(8,128)} fusion(f32[5,18,18,256]{3,0,2,1:T(8,128)} %get-tuple-element.300, f32[5,18,18,256]{3,0,2,1:T(8,128)} %copy-done, f32[5,18,18,256]{3,0,2,1:T(8,128)S(1)} %bitcast_convert_fusion.2, f32[5,18,18,256]{3,0,2,1:T(8,128)} %get-tuple-element.301, f32[5,18,18,256]{3,0,2,1:T(8,128)} %get-tuple-element.302, ...), kind=kLoop, calls=%fused_computation.6.clone.1 | loop fusion | flops 6881280 | bytes 22282244 | tf_op jit(solution)/shard_map/while/body/eval_jaxpr/add | solution.py:73
  328.8 4.5 fusion.75
  338.6 7.6 convert_multiply_fusion.3
  346.9 13.5 %fusion.76 = f32[5,16,16,256]{3,0,2,1:T(8,128)} fusion(f32[5,18,18,256]{3,0,2,1:T(8,128)} %get-tuple-element.300, f32[5,18,18,256]{3,0,2,1:T(8,128)} %copy-done, f32[5,18,18,256]{3,0,2,1:T(8,128)S(1)} %bitcast_convert_fusion.2, f32[5,18,18,256]{3,0,2,1:T(8,128)} %get-tuple-element.301, f32[5,18,18,256]{3,0,2,1:T(8,128)} %get-tuple-element.302, ...), kind=kLoop, calls=%fused_computation.6.clone.1 | loop fusion | flops 6881280 | bytes 22282244 | tf_op jit(solution)/shard_map/while/body/eval_jaxpr/add | solution.py:73
  368.2 4.5 fusion.75
  378.0 7.6 convert_multiply_fusion.3
  386.3 13.5 %fusion.76 = f32[5,16,16,256]{3,0,2,1:T(8,128)} fusion(f32[5,18,18,256]{3,0,2,1:T(8,128)} %get-tuple-element.300, f32[5,18,18,256]{3,0,2,1:T(8,128)} %copy-done, f32[5,18,18,256]{3,0,2,1:T(8,128)S(1)} %bitcast_convert_fusion.2, f32[5,18,18,256]{3,0,2,1:T(8,128)} %get-tuple-element.301, f32[5,18,18,256]{3,0,2,1:T(8,128)} %get-tuple-element.302, ...), kind=kLoop, calls=%fused_computation.6.clone.1 | loop fusion | flops 6881280 | bytes 22282244 | tf_op jit(solution)/shard_map/while/body/eval_jaxpr/add | solution.py:73
  407.6 4.5 fusion.75
  417.4 7.6 convert_multiply_fusion.3
  425.7 13.5 %fusion.76 = f32[5,16,16,256]{3,0,2,1:T(8,128)} fusion(f32[5,18,18,256]{3,0,2,1:T(8,128)} %get-tuple-element.300, f32[5,18,18,256]{3,0,2,1:T(8,128)} %copy-done, f32[5,18,18,256]{3,0,2,1:T(8,128)S(1)} %bitcast_convert_fusion.2, f32[5,18,18,256]{3,0,2,1:T(8,128)} %get-tuple-element.301, f32[5,18,18,256]{3,0,2,1:T(8,128)} %get-tuple-element.302, ...), kind=kLoop, calls=%fused_computation.6.clone.1 | loop fusion | flops 6881280 | bytes 22282244 | tf_op jit(solution)/shard_map/while/body/eval_jaxpr/add | solution.py:73
  447.1 4.5 fusion.75
  456.8 7.6 convert_multiply_fusion.3
  465.1 13.5 %fusion.76 = f32[5,16,16,256]{3,0,2,1:T(8,128)} fusion(f32[5,18,18,256]{3,0,2,1:T(8,128)} %get-tuple-element.300, f32[5,18,18,256]{3,0,2,1:T(8,128)} %copy-done, f32[5,18,18,256]{3,0,2,1:T(8,128)S(1)} %bitcast_convert_fusion.2, f32[5,18,18,256]{3,0,2,1:T(8,128)} %get-tuple-element.301, f32[5,18,18,256]{3,0,2,1:T(8,128)} %get-tuple-element.302, ...), kind=kLoop, calls=%fused_computation.6.clone.1 | loop fusion | flops 6881280 | bytes 22282244 | tf_op jit(solution)/shard_map/while/body/eval_jaxpr/add | solution.py:73
  486.5 4.5 fusion.75
  496.3 7.6 convert_multiply_fusion.3
  504.6 13.5 %fusion.76 = f32[5,16,16,256]{3,0,2,1:T(8,128)} fusion(f32[5,18,18,256]{3,0,2,1:T(8,128)} %get-tuple-element.300, f32[5,18,18,256]{3,0,2,1:T(8,128)} %copy-done, f32[5,18,18,256]{3,0,2,1:T(8,128)S(1)} %bitcast_convert_fusion.2, f32[5,18,18,256]{3,0,2,1:T(8,128)} %get-tuple-element.301, f32[5,18,18,256]{3,0,2,1:T(8,128)} %get-tuple-element.302, ...), kind=kLoop, calls=%fused_computation.6.clone.1 | loop fusion | flops 6881280 | bytes 22282244 | tf_op jit(solution)/shard_map/while/body/eval_jaxpr/add | solution.py:73
  525.9 4.5 fusion.75
  535.7 7.6 convert_multiply_fusion.3
  544.0 13.5 %fusion.76 = f32[5,16,16,256]{3,0,2,1:T(8,128)} fusion(f32[5,18,18,256]{3,0,2,1:T(8,128)} %get-tuple-element.300, f32[5,18,18,256]{3,0,2,1:T(8,128)} %copy-done, f32[5,18,18,256]{3,0,2,1:T(8,128)S(1)} %bitcast_convert_fusion.2, f32[5,18,18,256]{3,0,2,1:T(8,128)} %get-tuple-element.301, f32[5,18,18,256]{3,0,2,1:T(8,128)} %get-tuple-element.302, ...), kind=kLoop, calls=%fused_computation.6.clone.1 | loop fusion | flops 6881280 | bytes 22282244 | tf_op jit(solution)/shard_map/while/body/eval_jaxpr/add | solution.py:73
  565.3 4.5 fusion.75
  575.1 7.6 convert_multiply_fusion.3
  583.4 13.5 %fusion.76 = f32[5,16,16,256]{3,0,2,1:T(8,128)} fusion(f32[5,18,18,256]{3,0,2,1:T(8,128)} %get-tuple-element.300, f32[5,18,18,256]{3,0,2,1:T(8,128)} %copy-done, f32[5,18,18,256]{3,0,2,1:T(8,128)S(1)} %bitcast_convert_fusion.2, f32[5,18,18,256]{3,0,2,1:T(8,128)} %get-tuple-element.301, f32[5,18,18,256]{3,0,2,1:T(8,128)} %get-tuple-element.302, ...), kind=kLoop, calls=%fused_computation.6.clone.1 | loop fusion | flops 6881280 | bytes 22282244 | tf_op jit(solution)/shard_map/while/body/eval_jaxpr/add | solution.py:73
  614.6 7.6 convert_multiply_fusion.3
  622.9 13.5 %fusion.76 = f32[5,16,16,256]{3,0,2,1:T(8,128)} fusion(f32[5,18,18,256]{3,0,2,1:T(8,128)} %get-tuple-element.300, f32[5,18,18,256]{3,0,2,1:T(8,128)} %copy-done, f32[5,18,18,256]{3,0,2,1:T(8,128)S(1)} %bitcast_convert_fusion.2, f32[5,18,18,256]{3,0,2,1:T(8,128)} %get-tuple-element.301, f32[5,18,18,256]{3,0,2,1:T(8,128)} %get-tuple-element.302, ...), kind=kLoop, calls=%fused_computation.6.clone.1 | loop fusion | flops 6881280 | bytes 22282244 | tf_op jit(solution)/shard_map/while/body/eval_jaxpr/add | solution.py:73
  644.2 4.5 fusion.75
  654.0 7.6 convert_multiply_fusion.3
  662.3 13.5 %fusion.76 = f32[5,16,16,256]{3,0,2,1:T(8,128)} fusion(f32[5,18,18,256]{3,0,2,1:T(8,128)} %get-tuple-element.300, f32[5,18,18,256]{3,0,2,1:T(8,128)} %copy-done, f32[5,18,18,256]{3,0,2,1:T(8,128)S(1)} %bitcast_convert_fusion.2, f32[5,18,18,256]{3,0,2,1:T(8,128)} %get-tuple-element.301, f32[5,18,18,256]{3,0,2,1:T(8,128)} %get-tuple-element.302, ...), kind=kLoop, calls=%fused_computation.6.clone.1 | loop fusion | flops 6881280 | bytes 22282244 | tf_op jit(solution)/shard_map/while/body/eval_jaxpr/add | solution.py:73
  693.4 7.6 convert_multiply_fusion.3
  701.7 13.5 %fusion.76 = f32[5,16,16,256]{3,0,2,1:T(8,128)} fusion(f32[5,18,18,256]{3,0,2,1:T(8,128)} %get-tuple-element.300, f32[5,18,18,256]{3,0,2,1:T(8,128)} %copy-done, f32[5,18,18,256]{3,0,2,1:T(8,128)S(1)} %bitcast_convert_fusion.2, f32[5,18,18,256]{3,0,2,1:T(8,128)} %get-tuple-element.301, f32[5,18,18,256]{3,0,2,1:T(8,128)} %get-tuple-element.302, ...), kind=kLoop, calls=%fused_computation.6.clone.1 | loop fusion | flops 6881280 | bytes 22282244 | tf_op jit(solution)/shard_map/while/body/eval_jaxpr/add | solution.py:73
  723.1 4.5 fusion.75
  732.8 7.6 convert_multiply_fusion.3
  741.1 13.5 %fusion.76 = f32[5,16,16,256]{3,0,2,1:T(8,128)} fusion(f32[5,18,18,256]{3,0,2,1:T(8,128)} %get-tuple-element.300, f32[5,18,18,256]{3,0,2,1:T(8,128)} %copy-done, f32[5,18,18,256]{3,0,2,1:T(8,128)S(1)} %bitcast_convert_fusion.2, f32[5,18,18,256]{3,0,2,1:T(8,128)} %get-tuple-element.301, f32[5,18,18,256]{3,0,2,1:T(8,128)} %get-tuple-element.302, ...), kind=kLoop, calls=%fused_computation.6.clone.1 | loop fusion | flops 6881280 | bytes 22282244 | tf_op jit(solution)/shard_map/while/body/eval_jaxpr/add | solution.py:73
  772.3 7.6 convert_multiply_fusion.3
  780.6 13.5 %fusion.76 = f32[5,16,16,256]{3,0,2,1:T(8,128)} fusion(f32[5,18,18,256]{3,0,2,1:T(8,128)} %get-tuple-element.300, f32[5,18,18,256]{3,0,2,1:T(8,128)} %copy-done, f32[5,18,18,256]{3,0,2,1:T(8,128)S(1)} %bitcast_convert_fusion.2, f32[5,18,18,256]{3,0,2,1:T(8,128)} %get-tuple-element.301, f32[5,18,18,256]{3,0,2,1:T(8,128)} %get-tuple-element.302, ...), kind=kLoop, calls=%fused_computation.6.clone.1 | loop fusion | flops 6881280 | bytes 22282244 | tf_op jit(solution)/shard_map/while/body/eval_jaxpr/add | solution.py:73
  811.7 7.6 convert_multiply_fusion.3
  820.0 13.5 %fusion.76 = f32[5,16,16,256]{3,0,2,1:T(8,128)} fusion(f32[5,18,18,256]{3,0,2,1:T(8,128)} %get-tuple-element.300, f32[5,18,18,256]{3,0,2,1:T(8,128)} %copy-done, f32[5,18,18,256]{3,0,2,1:T(8,128)S(1)} %bitcast_convert_fusion.2, f32[5,18,18,256]{3,0,2,1:T(8,128)} %get-tuple-element.301, f32[5,18,18,256]{3,0,2,1:T(8,128)} %get-tuple-element.302, ...), kind=kLoop, calls=%fused_computation.6.clone.1 | loop fusion | flops 6881280 | bytes 22282244 | tf_op jit(solution)/shard_map/while/body/eval_jaxpr/add | solution.py:73
  851.1 7.6 convert_multiply_fusion.3
  859.4 13.5 %fusion.76 = f32[5,16,16,256]{3,0,2,1:T(8,128)} fusion(f32[5,18,18,256]{3,0,2,1:T(8,128)} %get-tuple-element.300, f32[5,18,18,256]{3,0,2,1:T(8,128)} %copy-done, f32[5,18,18,256]{3,0,2,1:T(8,128)S(1)} %bitcast_convert_fusion.2, f32[5,18,18,256]{3,0,2,1:T(8,128)} %get-tuple-element.301, f32[5,18,18,256]{3,0,2,1:T(8,128)} %get-tuple-element.302, ...), kind=kLoop, calls=%fused_computation.6.clone.1 | loop fusion | flops 6881280 | bytes 22282244 | tf_op jit(solution)/shard_map/while/body/eval_jaxpr/add | solution.py:73
  884.3 4.8 collective-permute-start.10
  895.4 7.0 collective-permute-start.12
  904.3 9.1 collective-permute-start.14
  917.9 7.1 collective-permute-done.15
  925.0 5.4 fusion.40
  930.4 9.4 fusion.32
  959.3 9.1 collective-permute-done.19
  970.9 5.4 fusion.38
  976.4 8.6 fusion.26
  (240 shorter events, 305.8 us)
Async XLA Ops:
  0.0 16.0 %copy-start.4 = (f32[5,16,16,256]{3,2,1,0:T(8,128)S(1)}, f32[5,16,16,256]{3,2,1,0:T(8,128)}, u32[]{:S(2)}) copy-start(f32[5,16,16,256]{3,2,1,0:T(8,128)} %param.10) | copy-start | bytes 3932164
  2.3 128.0 %collective-permute-start.6 = (bf16[16,5,1,16,256]{4,3,2,1,0:T(8,128)(2,1)}, bf16[16,5,1,16,256]{4,3,2,1,0:T(8,128)(2,1)}, u32[]{:S(2)}, u32[]{:S(2)}) collective-permute-start(bf16[16,5,1,16,256]{4,3,2,1,0:T(8,128)(2,1)} %get-tuple-element.204), channel_id=1, source_target_pairs={{0,32},{32,64},{64,96},{1,33},{33,65},{65,97},{2,34},{34,66},{66,9... | collective-permute-start | bytes 1966088 | tf_op jit(solution)/shard_map/ppermute | solution.py:15
  6.0 146.3 %collective-permute-start.7 = (bf16[16,5,1,16,256]{4,3,2,1,0:T(8,128)(2,1)S(1)}, bf16[16,5,1,16,256]{4,3,2,1,0:T(8,128)(2,1)}, u32[]{:S(2)}, u32[]{:S(2)}) collective-permute-start(bf16[16,5,1,16,256]{4,3,2,1,0:T(8,128)(2,1)S(1)} %get-tuple-element.203), channel_id=1, source_target_pairs={{32,0},{64,32},{96,64},{33,1},{65,33},{97,65},{34,2},{66,34},{98,6... | collective-permute-start | bytes 1966088 | tf_op jit(solution)/shard_map/ppermute | solution.py:17
  10.4 157.1 %collective-permute-start.2 = (bf16[16,5,1,16,256]{4,3,2,1,0:T(8,128)(2,1)}, bf16[16,5,1,16,256]{4,3,2,1,0:T(8,128)(2,1)}, u32[]{:S(2)}, u32[]{:S(2)}) collective-permute-start(bf16[16,5,1,16,256]{4,3,2,1,0:T(8,128)(2,1)} %get-tuple-element.206), channel_id=1, source_target_pairs={{0,32},{32,64},{64,96},{1,33},{33,65},{65,97},{2,34},{34,66},{66,9... | collective-permute-start | bytes 1966088 | tf_op jit(solution)/shard_map/ppermute | solution.py:15
  14.1 175.1 %collective-permute-start.3 = (bf16[16,5,1,16,256]{4,3,2,1,0:T(8,128)(2,1)}, bf16[16,5,1,16,256]{4,3,2,1,0:T(8,128)(2,1)}, u32[]{:S(2)}, u32[]{:S(2)}) collective-permute-start(bf16[16,5,1,16,256]{4,3,2,1,0:T(8,128)(2,1)} %get-tuple-element.205), channel_id=1, source_target_pairs={{32,0},{64,32},{96,64},{33,1},{65,33},{97,65},{34,2},{66,34},{98,6... | collective-permute-start | bytes 1966088 | tf_op jit(solution)/shard_map/ppermute | solution.py:17
  16.9 94.0 %copy-start.1 = (f32[5,16,16,256]{3,0,2,1:T(8,128)}, f32[5,16,16,256]{3,0,2,1:T(8,128)S(1)}, u32[]{:S(2)}) copy-start(f32[5,16,16,256]{3,0,2,1:T(8,128)S(1)} %copy.42) | copy-start | bytes 3932164
  17.6 95.0 %collective-permute-start.1 = (f32[5,1,16,256]{3,0,2,1:T(8,128)S(1)}, f32[5,1,16,256]{3,0,2,1:T(8,128)S(1)}, u32[]{:S(2)}, u32[]{:S(2)}) collective-permute-start(f32[5,1,16,256]{3,0,2,1:T(8,128)S(1)} %get-tuple-element.232), channel_id=1, source_target_pairs={{0,32},{32,64},{64,96},{1,33},{33,65},{65,97},{2,34},{34,66},{66,9... | collective-permute-start | bytes 245768 | tf_op jit(solution)/shard_map/ppermute | solution.py:15
  27.5 2.7 copy-start.15
  110.8 1.7 copy-start.16
  112.6 39.8 %copy-start.12 = (f32[5,1,16,256]{3,0,2,1:T(8,128)}, f32[5,1,16,256]{3,0,2,1:T(8,128)S(1)}, u32[]{:S(2)}) copy-start(f32[5,1,16,256]{3,0,2,1:T(8,128)S(1)} %collective-permute-done.1) | copy-start | bytes 245764
  112.6 778.4 %collective-permute-start = (f32[5,1,16,256]{3,0,2,1:T(8,128)}, f32[5,1,16,256]{3,0,2,1:T(8,128)}, u32[]{:S(2)}, u32[]{:S(2)}) collective-permute-start(f32[5,1,16,256]{3,0,2,1:T(8,128)} %get-tuple-element.231), channel_id=1, source_target_pairs={{32,0},{64,32},{96,64},{33,1},{65,33},{97,65},{34,2},{66,34},{98,6... | collective-permute-start | bytes 245768 | tf_op jit(solution)/shard_map/ppermute | solution.py:17
  156.0 47.8 %collective-permute-start.8 = (bf16[16,5,18,1,256]{4,0,3,2,1:T(8,128)(2,1)S(1)}, bf16[16,5,18,1,256]{4,0,3,2,1:T(8,128)(2,1)S(1)}, u32[]{:S(2)}, u32[]{:S(2)}) collective-permute-start(bf16[16,5,18,1,256]{4,0,3,2,1:T(8,128)(2,1)S(1)} %get-tuple-element.199), channel_id=1, source_target_pairs={{0,1},{1,2},{2,3},{3,4},{4,5},{5,6},{6,7},{7,8},{8,9},{9,10},{10,1... | collective-permute-start | bytes 2211848 | tf_op jit(solution)/shard_map/ppermute | solution.py:15
  165.6 38.2 %collective-permute-start.9 = (bf16[16,5,18,1,256]{4,0,3,2,1:T(8,128)(2,1)S(1)}, bf16[16,5,18,1,256]{4,0,3,2,1:T(8,128)(2,1)S(1)}, u32[]{:S(2)}, u32[]{:S(2)}) collective-permute-start(bf16[16,5,18,1,256]{4,0,3,2,1:T(8,128)(2,1)S(1)} %get-tuple-element.200), channel_id=1, source_target_pairs={{1,0},{2,1},{3,2},{4,3},{5,4},{6,5},{7,6},{8,7},{9,8},{10,9},{11,1... | collective-permute-start | bytes 2211848 | tf_op jit(solution)/shard_map/ppermute | solution.py:17
  192.8 32.4 %collective-permute-start.4 = (bf16[16,5,18,1,256]{4,0,3,2,1:T(8,128)(2,1)S(1)}, bf16[16,5,18,1,256]{4,0,3,2,1:T(8,128)(2,1)S(1)}, u32[]{:S(2)}, u32[]{:S(2)}) collective-permute-start(bf16[16,5,18,1,256]{4,0,3,2,1:T(8,128)(2,1)S(1)} %get-tuple-element.201), channel_id=1, source_target_pairs={{0,1},{1,2},{2,3},{3,4},{4,5},{5,6},{6,7},{7,8},{8,9},{9,10},{10,1... | collective-permute-start | bytes 2211848 | tf_op jit(solution)/shard_map/ppermute | solution.py:15
  201.9 25.5 %collective-permute-start.5 = (bf16[16,5,18,1,256]{4,0,3,2,1:T(8,128)(2,1)S(1)}, bf16[16,5,18,1,256]{4,0,3,2,1:T(8,128)(2,1)S(1)}, u32[]{:S(2)}, u32[]{:S(2)}) collective-permute-start(bf16[16,5,18,1,256]{4,0,3,2,1:T(8,128)(2,1)S(1)} %get-tuple-element.202), channel_id=1, source_target_pairs={{1,0},{2,1},{3,2},{4,3},{5,4},{6,5},{7,6},{8,7},{9,8},{10,9},{11,1... | collective-permute-start | bytes 2211848 | tf_op jit(solution)/shard_map/ppermute | solution.py:17
  203.8 23.5 %slice-start = ((s8[11796480]{0:T(1024)(128)(4,1)}), s8[4194304]{0:T(1024)(128)(4,1)S(1)}, s32[]{:S(2)}) async-start(s8[11796480]{0:T(1024)(128)(4,1)} %bitcast.119), calls=%async_computation | async-start | bytes 8388608
  203.8 23.5 %slice-start.1 = ((s8[11796480]{0:T(1024)(128)(4,1)}), s8[4194304]{0:T(1024)(128)(4,1)S(1)}, s32[]{:S(2)}) async-start(s8[11796480]{0:T(1024)(128)(4,1)} %bitcast.119), calls=%async_computation.1 | async-start | bytes 8388608
  211.6 15.7 %slice-start.2 = ((s8[11796480]{0:T(1024)(128)(4,1)}), s8[3407872]{0:T(1024)(128)(4,1)S(1)}, s32[]{:S(2)}) async-start(s8[11796480]{0:T(1024)(128)(4,1)} %bitcast.119), calls=%async_computation.2 | async-start | bytes 6815744
  229.1 13.5 %copy-start.17 = (s32[16]{0:T(128)S(1)}, s32[16]{0:T(128)}, u32[]{:S(2)}) copy-start(s32[16]{0:T(128)} %param.12) | copy-start | bytes 196
  242.7 630.4 %copy-start.14 = (f32[16,16,256]{2,1,0:T(8,128)S(1)}, f32[16,16,256]{2,1,0:T(8,128)}, u32[]{:S(2)}) copy-start(f32[16,16,256]{2,1,0:T(8,128)} %get-tuple-element.238) | copy-start | bytes 786436
  260.3 7.6 copy-start
  299.1 7.6 copy-start
  338.6 7.6 copy-start
  378.0 7.6 copy-start
  417.4 7.6 copy-start
  456.8 7.6 copy-start
  496.3 7.6 copy-start
  535.7 7.6 copy-start
  575.1 7.6 copy-start
  614.5 7.6 copy-start
  654.0 7.6 copy-start
  693.4 7.6 copy-start
  732.8 7.6 copy-start
  772.3 7.6 copy-start
  811.7 7.6 copy-start
  851.1 7.6 copy-start
  873.1 2.3 copy-start.3
  873.1 2.6 copy-start.5
  884.3 7.7 collective-permute-start.10
  889.1 6.3 collective-permute-start.11
  895.4 19.9 %collective-permute-start.12 = (f32[5,18,1,256]{3,0,2,1:T(8,128)S(1)}, f32[5,18,1,256]{3,0,2,1:T(8,128)S(1)}, u32[]{:S(2)}, u32[]{:S(2)}) collective-permute-start(f32[5,18,1,256]{3,0,2,1:T(8,128)S(1)} %get-tuple-element.215), channel_id=1, source_target_pairs={{0,1},{1,2},{2,3},{3,4},{4,5},{5,6},{6,7},{7,8},{8,9},{9,10},{10,1... | collective-permute-start | bytes 276488 | tf_op jit(solution)/shard_map/ppermute | solution.py:15
  902.4 13.0 %collective-permute-start.13 = (f32[5,18,1,256]{3,0,2,1:T(8,128)S(1)}, f32[5,18,1,256]{3,0,2,1:T(8,128)S(1)}, u32[]{:S(2)}, u32[]{:S(2)}) collective-permute-start(f32[5,18,1,256]{3,0,2,1:T(8,128)S(1)} %get-tuple-element.216), channel_id=1, source_target_pairs={{1,0},{2,1},{3,2},{4,3},{5,4},{6,5},{7,6},{8,7},{9,8},{10,9},{11,1... | collective-permute-start | bytes 276488 | tf_op jit(solution)/shard_map/ppermute | solution.py:17
  904.3 13.6 %collective-permute-start.14 = (f32[5,18,1,256]{3,0,2,1:T(8,128)S(1)}, f32[5,18,1,256]{3,0,2,1:T(8,128)S(1)}, u32[]{:S(2)}, u32[]{:S(2)}) collective-permute-start(f32[5,18,1,256]{3,0,2,1:T(8,128)S(1)} %get-tuple-element.213), channel_id=1, source_target_pairs={{0,1},{1,2},{2,3},{3,4},{4,5},{5,6},{6,7},{7,8},{8,9},{9,10},{10,1... | collective-permute-start | bytes 276488 | tf_op jit(solution)/shard_map/ppermute | solution.py:15
  913.4 11.6 %collective-permute-start.15 = (f32[5,18,1,256]{3,0,2,1:T(8,128)S(1)}, f32[5,18,1,256]{3,0,2,1:T(8,128)S(1)}, u32[]{:S(2)}, u32[]{:S(2)}) collective-permute-start(f32[5,18,1,256]{3,0,2,1:T(8,128)S(1)} %get-tuple-element.214), channel_id=1, source_target_pairs={{1,0},{2,1},{3,2},{4,3},{5,4},{6,5},{7,6},{8,7},{9,8},{10,9},{11,1... | collective-permute-start | bytes 276488 | tf_op jit(solution)/shard_map/ppermute | solution.py:17
  917.9 12.5 %copy-start.10 = (f32[5,18,18,256]{3,0,2,1:T(8,128)}, f32[5,18,18,256]{3,0,2,1:T(8,128)S(1)}, u32[]{:S(2)}) copy-start(f32[5,18,18,256]{3,0,2,1:T(8,128)S(1)} %convolution_bitcast_fusion.4) | copy-start | bytes 4976644
  917.9 12.5 %copy-start.2 = (f32[5,16,16,256]{3,0,2,1:T(8,128)S(1)}, f32[5,16,16,256]{3,0,2,1:T(8,128)}, u32[]{:S(2)}) copy-start(f32[5,16,16,256]{3,0,2,1:T(8,128)} %copy-done.1) | copy-start | bytes 3932164
  917.9 12.5 %copy-start.6 = (f32[5,16,16,255]{3,0,2,1:T(8,128)S(1)}, f32[5,16,16,255]{3,0,2,1:T(8,128)}, u32[]{:S(2)}) copy-start(f32[5,16,16,255]{3,0,2,1:T(8,128)} %get-tuple-element.223) | copy-start | bytes 3916804
  917.9 12.5 %copy-start.7 = (f32[5,16,16,255]{3,0,2,1:T(8,128)S(1)}, f32[5,16,16,255]{3,0,2,1:T(8,128)}, u32[]{:S(2)}) copy-start(f32[5,16,16,255]{3,0,2,1:T(8,128)} %get-tuple-element.224) | copy-start | bytes 3916804
  917.9 12.5 %copy-start.8 = (f32[5,16,16,1]{3,0,2,1:T(8,128)S(1)}, f32[5,16,16,1]{3,0,2,1:T(8,128)}, u32[]{:S(2)}) copy-start(f32[5,16,16,1]{3,0,2,1:T(8,128)} %get-tuple-element.225) | copy-start | bytes 15364
  917.9 12.5 %copy-start.9 = (f32[5,16,16,1]{3,0,2,1:T(8,128)S(1)}, f32[5,16,16,1]{3,0,2,1:T(8,128)}, u32[]{:S(2)}) copy-start(f32[5,16,16,1]{3,0,2,1:T(8,128)} %get-tuple-element.226) | copy-start | bytes 15364
  917.9 12.5 %copy-start.13 = (f32[5,1,16,256]{3,0,2,1:T(8,128)S(1)}, f32[5,1,16,256]{3,0,2,1:T(8,128)}, u32[]{:S(2)}) copy-start(f32[5,1,16,256]{3,0,2,1:T(8,128)} %copy-done.12) | copy-start | bytes 245764
  943.9 7.8 collective-permute-start.16
  947.1 6.3 collective-permute-start.17
  953.4 5.9 collective-permute-start.18
  956.8 11.6 %collective-permute-start.19 = (f32[5,18,1,256]{3,0,2,1:T(8,128)S(1)}, f32[5,18,1,256]{3,0,2,1:T(8,128)S(1)}, u32[]{:S(2)}, u32[]{:S(2)}) collective-permute-start(f32[5,18,1,256]{3,0,2,1:T(8,128)S(1)} %get-tuple-element.212), channel_id=1, source_target_pairs={{1,0},{2,1},{3,2},{4,3},{5,4},{6,5},{7,6},{8,7},{9,8},{10,9},{11,1... | collective-permute-start | bytes 276488 | tf_op jit(solution)/shard_map/ppermute | solution.py:17
  970.9 5.4 copy-start.11
